TPU v7x, 256 devices: a whole 4x4x8 slice. The times are simulated.
256 devices in a mesh: blk: 64 (over y, x_hi, z), orb: 4 (over x_lo, core).
Axes of the slice: x: 4 (x_hi: 2, x_lo: 2; x = x_hi * 2 + x_lo), y: 4, z: 8, core: 2. Of those that a mesh axis runs over, the one named last changes fastest.
Arguments:
- orbitals: bfloat16 [32768, 8192], P('blk', 'orb'), may hold values from -0.62890625 to 0.62890625
- coulomb_near: bfloat16 [32768, 512], P('blk'), may hold values from -0.52734375 to 0.52734375
- coulomb_far: bfloat16 [32768, 512], P('blk'), may hold values from -0.52734375 to 0.52734375
Outputs:
- exchange: bfloat16 [32768, 8192], P('blk', 'orb')
All inputs are finite; a program needn't handle non-finite values.
Results may differ from a plain program's by a relative error of at most 0.0049.
Values may be sent and summed in bfloat16 or wider, within the bound.
A program may use at most 64 MiB of HBM per device.

v0:
```python
import jax
import jax.numpy as jnp
from jax import lax
from jax.sharding import PartitionSpec as P


def from_behind(value, axis, by):
    devices = lax.axis_size(axis)
    return lax.ppermute(value, axis, [(i, (i + by) % devices) for i in range(devices)])


def weigh(partial_gram, slab):
    gram = lax.psum(partial_gram, "orb")
    return (gram * slab.astype(jnp.float32)).astype(jnp.bfloat16)


def contract_last(left, right):
    return lax.dot_general(
        left, right, (((1,), (1,)), ((), ())), preferred_element_type=jnp.float32
    )


def per_device(orbitals, coulomb_near, coulomb_far):
    far_offset = lax.axis_size("blk") // 4
    total = jnp.zeros(orbitals.shape, jnp.float32)
    for offset, slab in ((1, coulomb_near), (far_offset, coulomb_far)):
        partner_vals = from_behind(orbitals, "blk", -offset)
        weighted = weigh(contract_last(orbitals, partner_vals), slab)
        total = total + jnp.dot(weighted, partner_vals, preferred_element_type=jnp.float32)
        part = lax.dot_general(
            weighted, orbitals, (((0,), (0,)), ((), ())), preferred_element_type=jnp.float32
        )
        total = total + from_behind(part, "blk", offset)
    return total.astype(jnp.bfloat16)


def solution(mesh):
    return jax.shard_map(
        per_device,
        mesh=mesh,
        in_specs=(P("blk", "orb"), P("blk", None), P("blk", None)),
        out_specs=P("blk", "orb"),
        check_vma=False,
    )
```

profile of v0, /device:TPU:1, one launch (start us, length us, event | category | flops | bytes accessed | tf_op | source)
XLA Modules:
  0.0 369.2 jit_solution(7682520830236336286)
XLA Ops:
  6.5 0.0 all-reduce.3.cloned.1.call-start
  6.5 3.6 collective-permute-start.2
  10.1 8.2 %collective-permute-start = (bf16[512,2048]{1,0:T(8,128)(2,1)}, bf16[512,2048]{1,0:T(8,128)(2,1)S(1)}, u32[]{:S(2)}, u32[]{:S(2)}) collective-permute-start(bf16[512,2048]{1,0:T(8,128)(2,1)} %param.3), channel_id=1, source_target_pairs={{0,252},{4,0},{8,4},{12,8},{16,12},{20,16},{24,20},{28,24},{32,28}... | collective-permute-start | bytes 6291464 | tf_op jit(solution)/shard_map/ppermute | solution.py:9
  18.3 36.4 %collective-permute-done.2 = bf16[512,2048]{1,0:T(8,128)(2,1)S(1)} collective-permute-done((bf16[512,2048]{1,0:T(8,128)(2,1)}, bf16[512,2048]{1,0:T(8,128)(2,1)S(1)}, u32[]{:S(2)}, u32[]{:S(2)}) %collective-permute-start.2) | collective-permute-done | bytes 2097184 | tf_op jit(solution)/shard_map/ppermute | solution.py:9
  54.7 0.0 copy-start.3
  54.7 4.6 %fusion.5 = f32[512,512]{1,0:T(8,128)} fusion(bf16[512,2048]{1,0:T(8,128)(2,1)} %param.3, bf16[512,2048]{1,0:T(8,128)(2,1)S(1)} %collective-permute-done.2), kind=kOutput, calls=%fused_computation.8 | convolution fusion | flops 1073741824 | bytes 5242880 | tf_op jit(solution)/shard_map/dot_general | solution.py:18
  59.3 0.0 copy-done.3
  59.3 3.3 collective-permute-done
  62.7 0.0 copy-start.5
  62.7 1.3 copy-done.5
  64.0 0.0 copy-done
  64.0 2.3 fusion.4
  66.3 0.0 copy-start.7
  66.3 0.0 all-reduce.3.cloned.1.call-update
  66.3 107.4 %all-reduce.3.cloned.1.call-done = (f32[512,512]{1,0:T(8,128)}, f32[512,512]{1,0:T(8,128)}) async-done(((f32[512,512]{1,0:T(8,128)}, f32[512,512]{1,0:T(8,128)}), (f32[512,512]{1,0:T(8,128)}, f32[512,512]{1,0:T(8,128)})) %all-reduce.3.cloned.1.call-update) | async-done | bytes 2097168 | tf_op jit(solution)/shard_map/psum | solution.py:13
  173.7 0.0 copy-done.7
  173.7 0.0 copy-start.2
  173.7 2.7 fusion.2
  176.4 1.3 collective-permute-start.3
  177.7 0.0 copy-done.2
  177.7 0.0 copy-done.8
  177.7 1.3 fusion
  179.1 0.0 copy-start.1
  179.1 0.0 copy-start.4
  179.1 1.4 collective-permute-start.1
  180.4 0.0 copy-done.6
  180.4 1.3 fusion.1
  181.7 177.8 %collective-permute-done.3 = f32[512,2048]{1,0:T(8,128)S(1)} collective-permute-done((f32[512,2048]{1,0:T(8,128)S(1)}, f32[512,2048]{1,0:T(8,128)S(1)}, u32[]{:S(2)}, u32[]{:S(2)}) %collective-permute-start.3) | collective-permute-done | bytes 4194336 | tf_op jit(solution)/shard_map/ppermute | solution.py:9
  359.5 0.0 collective-permute-done.1
  359.5 0.0 copy-done.1
  359.5 0.0 copy-done.4
  359.5 2.8 add_convert_fusion
  (3 shorter events, 0.0 us)
Async XLA Ops:
  6.5 57.4 %copy-start = (bf16[512,2048]{1,0:T(8,128)(2,1)S(1)}, bf16[512,2048]{1,0:T(8,128)(2,1)}, u32[]{:S(2)}) copy-start(bf16[512,2048]{1,0:T(8,128)(2,1)} %param.3) | copy-start | bytes 6291460
  6.5 167.2 %all-reduce.3.cloned.1.call-start = ((), (), s32[]{:S(2)}) async-start(), calls=%async_computation | async-start | bytes 4194304 | tf_op jit(solution)/shard_map/psum | solution.py:13
  6.5 48.2 %collective-permute-start.2 = (bf16[512,2048]{1,0:T(8,128)(2,1)}, bf16[512,2048]{1,0:T(8,128)(2,1)S(1)}, u32[]{:S(2)}, u32[]{:S(2)}) collective-permute-start(bf16[512,2048]{1,0:T(8,128)(2,1)} %param.3), channel_id=1, source_target_pairs={{0,192},{4,196},{8,200},{12,204},{16,208},{20,212},{24,216},{28,22... | collective-permute-start | bytes 6291464 | tf_op jit(solution)/shard_map/ppermute | solution.py:9
  10.1 52.6 %collective-permute-start = (bf16[512,2048]{1,0:T(8,128)(2,1)}, bf16[512,2048]{1,0:T(8,128)(2,1)S(1)}, u32[]{:S(2)}, u32[]{:S(2)}) collective-permute-start(bf16[512,2048]{1,0:T(8,128)(2,1)} %param.3), channel_id=1, source_target_pairs={{0,252},{4,0},{8,4},{12,8},{16,12},{20,16},{24,20},{28,24},{32,28}... | collective-permute-start | bytes 6291464 | tf_op jit(solution)/shard_map/ppermute | solution.py:9
  54.7 4.6 %copy-start.3 = (bf16[512,2048]{1,0:T(8,128)(2,1)}, bf16[512,2048]{1,0:T(8,128)(2,1)S(1)}, u32[]{:S(2)}) copy-start(bf16[512,2048]{1,0:T(8,128)(2,1)S(1)} %collective-permute-done.2) | copy-start | bytes 6291460
  62.7 1.3 copy-start.5
  66.3 107.5 %copy-start.7 = (bf16[512,512]{1,0:T(8,128)(2,1)S(1)}, bf16[512,512]{1,0:T(8,128)(2,1)}, u32[]{:S(2)}) copy-start(bf16[512,512]{1,0:T(8,128)(2,1)} %param.5) | copy-start | bytes 1572868
  173.7 4.0 %copy-start.2 = (f32[512,512]{1,0:T(8,128)S(1)}, f32[512,512]{1,0:T(8,128)}, u32[]{:S(2)}) copy-start(f32[512,512]{1,0:T(8,128)} %get-tuple-element.6) | copy-start | bytes 3145732
  173.7 4.0 %copy-start.8 = (bf16[512,512]{1,0:T(8,128)(2,1)S(1)}, bf16[512,512]{1,0:T(8,128)(2,1)}, u32[]{:S(2)}) copy-start(bf16[512,512]{1,0:T(8,128)(2,1)} %param.4) | copy-start | bytes 1572868
  176.4 183.1 %collective-permute-start.3 = (f32[512,2048]{1,0:T(8,128)S(1)}, f32[512,2048]{1,0:T(8,128)S(1)}, u32[]{:S(2)}, u32[]{:S(2)}) collective-permute-start(f32[512,2048]{1,0:T(8,128)S(1)} %fusion.2), channel_id=1, source_target_pairs={{0,64},{4,68},{8,72},{12,76},{16,80},{20,84},{24,88},{28,92},{32,9... | collective-permute-start | bytes 12582920 | tf_op jit(solution)/shard_map/ppermute | solution.py:9
  177.7 2.7 copy-start.6
  179.1 180.5 %copy-start.1 = (f32[512,512]{1,0:T(8,128)S(1)}, f32[512,512]{1,0:T(8,128)}, u32[]{:S(2)}) copy-start(f32[512,512]{1,0:T(8,128)} %get-tuple-element.5) | copy-start | bytes 3145732
  179.1 180.5 %copy-start.4 = (bf16[512,2048]{1,0:T(8,128)(2,1)S(1)}, bf16[512,2048]{1,0:T(8,128)(2,1)}, u32[]{:S(2)}) copy-start(bf16[512,2048]{1,0:T(8,128)(2,1)} %copy-done.3) | copy-start | bytes 6291460
  179.1 180.5 %collective-permute-start.1 = (f32[512,2048]{1,0:T(8,128)S(1)}, f32[512,2048]{1,0:T(8,128)S(1)}, u32[]{:S(2)}, u32[]{:S(2)}) collective-permute-start(f32[512,2048]{1,0:T(8,128)S(1)} %fusion), channel_id=1, source_target_pairs={{0,4},{4,8},{8,12},{12,16},{16,20},{20,24},{24,28},{28,32},{32,36}... | collective-permute-start | bytes 12582920 | tf_op jit(solution)/shard_map/ppermute | solution.py:9
Sparse Core Ops, SparseCore 0:
  66.4 107.2 all-reduce.2
where the time goes:
time: 369 us
  waiting for transfers between devices  325 us (88%)
  matrix products  14.9 us (4%)
  starting transfers between devices  14.4 us (4%)
  between operations  13.4 us (4%)
    ppermute x4, waiting for transfers between devices, from_behind(): lax.ppermute(value, axis, [(i, (i + by) % devices) for i in range(devices)])  218 us
    psum x1, waiting for transfers between devices, weigh(): gram = lax.psum(partial_gram, 'orb')  107 us
    ppermute x4, starting transfers between devices, from_behind(): lax.ppermute(value, axis, [(i, (i + by) % devices) for i in range(devices)])  14.4 us
  transfers between devices with their start and end apart: 5, of which 4 were waited for; matrix products, arithmetic and copies ran while one was open for 2% of the time, Pallas kernels for 0%

commit v1 on v0

v1 whole, which is shorter than its diff:
```python
import jax
import jax.numpy as jnp
from jax import lax
from jax.sharding import PartitionSpec as P


def from_behind(value, axis, by):
    devices = lax.axis_size(axis)
    return lax.ppermute(value, axis, [(i, (i + by) % devices) for i in range(devices)])


def contract(left, right, dims):
    return lax.dot_general(left, right, (dims, ((), ())), preferred_element_type=jnp.float32)


def per_device(orbitals, coulomb_near, coulomb_far):
    far_offset = lax.axis_size("blk") // 4
    offsets = (far_offset, 1)
    slabs = (coulomb_far, coulomb_near)
    ahead = [from_behind(orbitals, "blk", -k) for k in offsets]
    behind = [from_behind(orbitals, "blk", k) for k in offsets]
    grams = [lax.psum(contract(orbitals, psi, ((1,), (1,))), "orb") for psi in ahead]
    weighted = [(g * v.astype(jnp.float32)).astype(jnp.bfloat16) for g, v in zip(grams, slabs)]
    arrived = [from_behind(w, "blk", k) for w, k in zip(weighted, offsets)]
    total = contract(weighted[0], ahead[0], ((1,), (0,)))
    total = total + contract(weighted[1], ahead[1], ((1,), (0,)))
    total = total + contract(arrived[0], behind[0], ((0,), (0,)))
    total = total + contract(arrived[1], behind[1], ((0,), (0,)))
    return total.astype(jnp.bfloat16)


def solution(mesh):
    return jax.shard_map(
        per_device,
        mesh=mesh,
        in_specs=(P("blk", "orb"), P("blk", None), P("blk", None)),
        out_specs=P("blk", "orb"),
        check_vma=False,
    )
```

time: 369 us -> 249 us (0.67)
  waiting for transfers between devices: 325 us -> 200 us
    ppermute x4 -> x6, waiting for transfers between devices: 218 us -> 60.2 us  [from_behind(): lax.ppermute(value, axis, [(i, (i + by) % devices) for i in range(devices)])]
    psum x1, waiting for transfers between devices: 107 us -> 140 us  [per_device(): lax.psum(contract(orbitals, psi, ((1,), (1,))), 'orb')]
    ppermute x4 -> x6, starting transfers between devices: 14.4 us -> 15.5 us  [from_behind(): lax.ppermute(value, axis, [(i, (i + by) % devices) for i in range(devices)])]
  transfers between devices with their start and end apart: 5 -> 7, of which waited for: 4 -> 4; matrix products, arithmetic and copies ran while one was open for 2% -> 5% of each run, Pallas kernels for 0% -> 0%
where the time goes in v1:
time: 249 us
  waiting for transfers between devices  200 us (80%)
  matrix products  17 us (7%)
  starting transfers between devices  15.5 us (6%)
  between operations  13.5 us (5%)
    psum x1, waiting for transfers between devices, per_device(): lax.psum(contract(orbitals, psi, ((1,), (1,))), 'orb')  140 us
    ppermute x6, waiting for transfers between devices, from_behind(): lax.ppermute(value, axis, [(i, (i + by) % devices) for i in range(devices)])  60.2 us
    dot_general x6, matrix products, contract(): lax.dot_general(left, right, (dims, ((), ())), preferred_element_type=jnp...  17 us
    ppermute x6, starting transfers between devices, from_behind(): lax.ppermute(value, axis, [(i, (i + by) % devices) for i in range(devices)])  15.5 us
  transfers between devices with their start and end apart: 7, of which 4 were waited for; matrix products, arithmetic and copies ran while one was open for 5% of the time, Pallas kernels for 0%

profile of v1, /device:TPU:1, one launch (start us, length us, event | category | flops | bytes accessed | tf_op | source)
XLA Modules:
  0.0 249.2 jit_solution(10841993827190040357)
XLA Ops:
  6.5 0.0 all-reduce.3.cloned.1.call-start
  6.5 3.6 %collective-permute-start = (bf16[512,2048]{1,0:T(8,128)(2,1)}, bf16[512,2048]{1,0:T(8,128)(2,1)S(1)}, u32[]{:S(2)}, u32[]{:S(2)}) collective-permute-start(bf16[512,2048]{1,0:T(8,128)(2,1)} %param.3), channel_id=1, source_target_pairs={{0,192},{4,196},{8,200},{12,204},{16,208},{20,212},{24,216},{28,22... | collective-permute-start | bytes 6291464 | tf_op jit(solution)/shard_map/ppermute | solution.py:9
  10.1 8.2 %collective-permute-start.1 = (bf16[512,2048]{1,0:T(8,128)(2,1)}, bf16[512,2048]{1,0:T(8,128)(2,1)S(1)}, u32[]{:S(2)}, u32[]{:S(2)}) collective-permute-start(bf16[512,2048]{1,0:T(8,128)(2,1)} %param.3), channel_id=1, source_target_pairs={{0,252},{4,0},{8,4},{12,8},{16,12},{20,16},{24,20},{28,24},{32,28}... | collective-permute-start | bytes 6291464 | tf_op jit(solution)/shard_map/ppermute | solution.py:9
  18.3 36.4 %collective-permute-done = bf16[512,2048]{1,0:T(8,128)(2,1)S(1)} collective-permute-done((bf16[512,2048]{1,0:T(8,128)(2,1)}, bf16[512,2048]{1,0:T(8,128)(2,1)S(1)}, u32[]{:S(2)}, u32[]{:S(2)}) %collective-permute-start) | collective-permute-done | bytes 2097184 | tf_op jit(solution)/shard_map/ppermute | solution.py:9
  54.7 0.0 copy-start
  54.7 4.6 %fusion = f32[512,512]{1,0:T(8,128)} fusion(bf16[512,2048]{1,0:T(8,128)(2,1)} %param.3, bf16[512,2048]{1,0:T(8,128)(2,1)S(1)} %collective-permute-done), kind=kOutput, calls=%fused_computation.3 | convolution fusion | flops 1073741824 | bytes 5242880 | tf_op jit(solution)/shard_map/dot_general | solution.py:13
  59.3 0.0 copy-done
  59.3 3.3 %collective-permute-done.1 = bf16[512,2048]{1,0:T(8,128)(2,1)S(1)} collective-permute-done((bf16[512,2048]{1,0:T(8,128)(2,1)}, bf16[512,2048]{1,0:T(8,128)(2,1)S(1)}, u32[]{:S(2)}, u32[]{:S(2)}) %collective-permute-start.1) | collective-permute-done | bytes 2097184 | tf_op jit(solution)/shard_map/ppermute | solution.py:9
  62.7 1.3 copy-done.2
  64.0 3.9 %fusion.2 = f32[512,512]{1,0:T(8,128)} fusion(bf16[512,2048]{1,0:T(8,128)(2,1)} %param.3, bf16[512,2048]{1,0:T(8,128)(2,1)S(1)} %collective-permute-done.1), kind=kOutput, calls=%fused_computation.5 | convolution fusion | flops 1073741824 | bytes 5242880 | tf_op jit(solution)/shard_map/dot_general | solution.py:13
  67.9 0.0 all-reduce.3.cloned.1.call-update
  67.9 1.1 collective-permute-start.3
  69.0 0.0 collective-permute-start.5
  69.0 140.0 %all-reduce.3.cloned.1.call-done = (f32[512,512]{1,0:T(8,128)}, f32[512,512]{1,0:T(8,128)}) async-done(((f32[512,512]{1,0:T(8,128)}, f32[512,512]{1,0:T(8,128)}), (f32[512,512]{1,0:T(8,128)}, f32[512,512]{1,0:T(8,128)})) %all-reduce.3.cloned.1.call-update) | async-done | bytes 2097168 | tf_op jit(solution)/shard_map/psum | solution.py:22
  209.0 0.0 copy-done.5
  209.0 1.5 multiply_convert_fusion.1
  210.6 1.3 collective-permute-start.2
  211.9 0.0 copy-done.6
  211.9 0.0 copy-done.4
  211.9 0.2 multiply_convert_fusion
  212.0 0.0 copy-start.3
  212.0 1.4 collective-permute-start.4
  213.4 0.0 copy-done.1
  213.4 1.3 fusion.1
  214.6 0.0 copy-done.3
  214.7 1.3 fusion.3
  215.9 0.0 collective-permute-done.3
  215.9 20.5 %collective-permute-done.2 = bf16[512,512]{1,0:T(8,128)(2,1)S(1)} collective-permute-done((bf16[512,512]{1,0:T(8,128)(2,1)S(1)}, bf16[512,512]{1,0:T(8,128)(2,1)S(1)}, u32[]{:S(2)}, u32[]{:S(2)}) %collective-permute-start.2) | collective-permute-done | bytes 524320 | tf_op jit(solution)/shard_map/ppermute | solution.py:9
  236.4 2.9 %fusion.4 = f32[512,2048]{1,0:T(8,128)S(1)} fusion(bf16[512,512]{1,0:T(8,128)(2,1)S(1)} %collective-permute-done.2, bf16[512,2048]{1,0:T(8,128)(2,1)} %collective-permute-done.3), kind=kOutput, calls=%fused_computation.7 | convolution fusion | flops 1073741824 | bytes 6815744 | tf_op jit(solution)/shard_map/dot_general | solution.py:13
  239.3 0.0 collective-permute-done.5
  239.3 0.0 collective-permute-done.4
  239.3 3.1 %add_convert_fusion = bf16[512,2048]{1,0:T(8,128)(2,1)} fusion(f32[512,2048]{1,0:T(8,128)S(1)} %fusion.4, f32[512,2048]{1,0:T(8,128)S(1)} %fusion.1, f32[512,2048]{1,0:T(8,128)S(1)} %fusion.3, bf16[512,512]{1,0:T(8,128)(2,1)S(1)} %collective-permute-done.4, bf16[512,2048]{1,0:T(8,128)(2,1)S(1)} %collective-permute-done.5), kind=kOutput, calls=%fused_computation | convolution fusion | flops 1077936128 | bytes 17301504 | tf_op jit(solution)/shard_map/dot_general | solution.py:13
  (5 shorter events, 0.0 us)
Async XLA Ops:
  6.5 202.5 %all-reduce.3.cloned.1.call-start = ((), (), s32[]{:S(2)}) async-start(), calls=%async_computation | async-start | bytes 4194304 | tf_op jit(solution)/shard_map/psum | solution.py:22
  6.5 48.2 %collective-permute-start = (bf16[512,2048]{1,0:T(8,128)(2,1)}, bf16[512,2048]{1,0:T(8,128)(2,1)S(1)}, u32[]{:S(2)}, u32[]{:S(2)}) collective-permute-start(bf16[512,2048]{1,0:T(8,128)(2,1)} %param.3), channel_id=1, source_target_pairs={{0,192},{4,196},{8,200},{12,204},{16,208},{20,212},{24,216},{28,22... | collective-permute-start | bytes 6291464 | tf_op jit(solution)/shard_map/ppermute | solution.py:9
  10.1 52.6 %collective-permute-start.1 = (bf16[512,2048]{1,0:T(8,128)(2,1)}, bf16[512,2048]{1,0:T(8,128)(2,1)S(1)}, u32[]{:S(2)}, u32[]{:S(2)}) collective-permute-start(bf16[512,2048]{1,0:T(8,128)(2,1)} %param.3), channel_id=1, source_target_pairs={{0,252},{4,0},{8,4},{12,8},{16,12},{20,16},{24,20},{28,24},{32,28}... | collective-permute-start | bytes 6291464 | tf_op jit(solution)/shard_map/ppermute | solution.py:9
  54.7 4.6 %copy-start = (bf16[512,2048]{1,0:T(8,128)(2,1)}, bf16[512,2048]{1,0:T(8,128)(2,1)S(1)}, u32[]{:S(2)}) copy-start(bf16[512,2048]{1,0:T(8,128)(2,1)S(1)} %collective-permute-done) | copy-start | bytes 6291460
  62.7 1.3 copy-start.2
  67.9 141.1 %copy-start.5 = (bf16[512,512]{1,0:T(8,128)(2,1)S(1)}, bf16[512,512]{1,0:T(8,128)(2,1)}, u32[]{:S(2)}) copy-start(bf16[512,512]{1,0:T(8,128)(2,1)} %param.5) | copy-start | bytes 1572868
  67.9 144.0 %copy-start.6 = (bf16[512,512]{1,0:T(8,128)(2,1)S(1)}, bf16[512,512]{1,0:T(8,128)(2,1)}, u32[]{:S(2)}) copy-start(bf16[512,512]{1,0:T(8,128)(2,1)} %param.4) | copy-start | bytes 1572868
  67.9 148.0 %collective-permute-start.3 = (bf16[512,2048]{1,0:T(8,128)(2,1)}, bf16[512,2048]{1,0:T(8,128)(2,1)}, u32[]{:S(2)}, u32[]{:S(2)}) collective-permute-start(bf16[512,2048]{1,0:T(8,128)(2,1)} %param.3), channel_id=1, source_target_pairs={{0,64},{4,68},{8,72},{12,76},{16,80},{20,84},{24,88},{28,92},{32,9... | collective-permute-start | bytes 6291464 | tf_op jit(solution)/shard_map/ppermute | solution.py:9
  69.0 170.3 %collective-permute-start.5 = (bf16[512,2048]{1,0:T(8,128)(2,1)}, bf16[512,2048]{1,0:T(8,128)(2,1)S(1)}, u32[]{:S(2)}, u32[]{:S(2)}) collective-permute-start(bf16[512,2048]{1,0:T(8,128)(2,1)} %param.3), channel_id=1, source_target_pairs={{0,4},{4,8},{8,12},{12,16},{16,20},{20,24},{24,28},{28,32},{32,36}... | collective-permute-start | bytes 6291464 | tf_op jit(solution)/shard_map/ppermute | solution.py:9
  209.0 2.8 %copy-start.4 = (f32[512,512]{1,0:T(8,128)S(1)}, f32[512,512]{1,0:T(8,128)}, u32[]{:S(2)}) copy-start(f32[512,512]{1,0:T(8,128)} %get-tuple-element.5) | copy-start | bytes 3145732
  209.0 4.4 %copy-start.1 = (bf16[512,2048]{1,0:T(8,128)(2,1)S(1)}, bf16[512,2048]{1,0:T(8,128)(2,1)}, u32[]{:S(2)}) copy-start(bf16[512,2048]{1,0:T(8,128)(2,1)} %copy-done) | copy-start | bytes 6291460
  210.6 25.8 %collective-permute-start.2 = (bf16[512,512]{1,0:T(8,128)(2,1)S(1)}, bf16[512,512]{1,0:T(8,128)(2,1)S(1)}, u32[]{:S(2)}, u32[]{:S(2)}) collective-permute-start(bf16[512,512]{1,0:T(8,128)(2,1)S(1)} %multiply_convert_fusion.1), channel_id=1, source_target_pairs={{0,64},{4,68},{8,72},{12,76},{16,80},{20,84},{24,88},{28,92},{32,9... | collective-permute-start | bytes 1572872 | tf_op jit(solution)/shard_map/ppermute | solution.py:9
  212.0 2.6 %copy-start.3 = (bf16[512,2048]{1,0:T(8,128)(2,1)S(1)}, bf16[512,2048]{1,0:T(8,128)(2,1)}, u32[]{:S(2)}) copy-start(bf16[512,2048]{1,0:T(8,128)(2,1)} %copy-done.2) | copy-start | bytes 6291460
  212.0 27.3 %collective-permute-start.4 = (bf16[512,512]{1,0:T(8,128)(2,1)S(1)}, bf16[512,512]{1,0:T(8,128)(2,1)S(1)}, u32[]{:S(2)}, u32[]{:S(2)}) collective-permute-start(bf16[512,512]{1,0:T(8,128)(2,1)S(1)} %multiply_convert_fusion), channel_id=1, source_target_pairs={{0,4},{4,8},{8,12},{12,16},{16,20},{20,24},{24,28},{28,32},{32,36}... | collective-permute-start | bytes 1572872 | tf_op jit(solution)/shard_map/ppermute | solution.py:9
Sparse Core Ops, SparseCore 0:
  68.0 140.9 all-reduce.2

commit v2 on v1

v2 whole, which is shorter than its diff:
```python
import functools

import jax
import jax.numpy as jnp
from jax import lax
from jax.experimental import pallas as pl
from jax.experimental.pallas import tpu as pltpu
from jax.sharding import PartitionSpec as P

MESH = pl.DeviceIdType.MESH
PIECES = 8
CHUNKS = 4
FAR = 16
DEPTH = 8
DOWN, UP = 0, 1


def contract(left, right, dims):
    return lax.dot_general(left, right, (dims, ((), ())), preferred_element_type=jnp.float32)


def kernel(
    blocks,
    psi_hbm,
    near_hbm,
    far_hbm,
    out_hbm,
    own,
    taken,
    slab,
    gram,
    gram_in,
    half_out,
    half_in,
    weight,
    weight_in,
    total,
    result,
    load_sem,
    store_sem,
    psi_send,
    psi_recv,
    pair_send,
    pair_recv,
):
    rows, width = own.shape
    piece, chunk, half = rows // PIECES, rows // CHUNKS, rows // 2
    b, o = lax.axis_index("blk"), lax.axis_index("orb")
    z, x_hi = b % DEPTH, (b // DEPTH) % 2
    core = o % 2
    sibling, across = (b, o + 1 - 2 * core), (b, (o + 2) % 4)
    turned = b + DEPTH - 2 * DEPTH * x_hi
    low, high = 1 - (z + DEPTH - 1) // DEPTH, (z + 1) // DEPTH
    ahead = (((b + FAR) % blocks, o), ((b + 1) % blocks, o))
    behind = (((b + blocks - FAR) % blocks, o), ((b + blocks - 1) % blocks, o))
    near_down = ((1 - low) * behind[1][0] + low * (turned + DEPTH - 1), o)
    near_up = ((1 - high) * ahead[1][0] + high * (turned - DEPTH + 1), o)

    mine = pl.ds(pl.multiple_of(core * half, half), half)
    other = pl.ds(pl.multiple_of((1 - core) * half, half), half)

    def stream(offset, way, source, s):
        target = ((behind[0], ahead[0]), (near_down, near_up))[offset][way]
        part = pl.ds(pl.multiple_of(s * piece, piece), piece)
        return pltpu.make_async_remote_copy(
            src_ref=source.at[part],
            dst_ref=taken.at[offset, way, part],
            send_sem=psi_send.at[offset, way, s],
            recv_sem=psi_recv.at[offset, way, s],
            device_id=target,
            device_id_type=MESH,
        )

    def arrival(offset, way, s):
        part = pl.ds(pl.multiple_of(s * piece, piece), piece)
        return pltpu.make_async_remote_copy(
            src_ref=psi_hbm.at[part],
            dst_ref=taken.at[offset, way, part],
            send_sem=psi_send.at[offset, way, s],
            recv_sem=psi_recv.at[offset, way, s],
            device_id=sibling,
            device_id_type=MESH,
        )

    def pair(kind, offset, j, source, target, device):
        return pltpu.make_async_remote_copy(
            src_ref=source,
            dst_ref=target,
            send_sem=pair_send.at[kind, offset, j],
            recv_sem=pair_recv.at[kind, offset, j],
            device_id=device,
            device_id_type=MESH,
        )

    def gram_to_sibling(k, j):
        return pair(0, k, j, gram.at[k, j, other], gram_in.at[k, j], sibling)

    def half_across(k, j):
        return pair(1, k, j, half_out.at[k, j], half_in.at[k, j], across)

    def weight_to_sibling(k, j):
        return pair(2, k, j, weight.at[k, j, mine], weight.at[k, j, mine], sibling)

    def weight_ahead(k, j):
        block = (1 - k) * ahead[0][0] + k * ahead[1][0]
        return pair(3, k, j, weight.at[k, j, mine], weight_in.at[k, j, mine], (block, o))

    def weight_on(k, j):
        return pair(4, k, j, weight_in.at[k, j, mine], weight_in.at[k, j, mine], sibling)

    def columns(j):
        return pl.ds(pl.multiple_of(j * chunk, chunk), chunk)

    loads = [
        pltpu.make_async_copy(psi_hbm, own, load_sem.at[0]),
        pltpu.make_async_copy(far_hbm, slab.at[0], load_sem.at[1]),
        pltpu.make_async_copy(near_hbm, slab.at[1], load_sem.at[2]),
    ]
    for load in loads:
        load.start()

    barrier = pltpu.get_barrier_semaphore()
    peers = (sibling, across, ahead[0], behind[0], ahead[1], behind[1], near_down, near_up)
    for peer in peers:
        pl.semaphore_signal(barrier, inc=1, device_id=peer, device_id_type=MESH)
    pl.semaphore_wait(barrier, len(peers))

    for s in range(PIECES):
        stream(0, DOWN, psi_hbm, s).start()
        stream(0, UP, psi_hbm, s).start()

        @pl.when(z > 0)
        def _():
            stream(1, DOWN, psi_hbm, s).start()

        @pl.when(z < DEPTH - 1)
        def _():
            stream(1, UP, psi_hbm, s).start()

    @pl.when((z == 0) & (x_hi == 1))
    def _():
        stream(1, DOWN, psi_hbm, 0).start()

    @pl.when((z == DEPTH - 1) & (x_hi == 0))
    def _():
        stream(1, UP, psi_hbm, 0).start()

    total[...] = jnp.zeros_like(total)
    for load in loads:
        load.wait()

    def turn(s):
        @pl.when((z == 0) & (x_hi == 0))
        def _():
            stream(1, DOWN, taken.at[0, DOWN], s).start()

        @pl.when((z == 0) & (x_hi == 1) & (s < PIECES - 1))
        def _():
            stream(1, DOWN, psi_hbm, s + 1).start()

        @pl.when((z == DEPTH - 1) & (x_hi == 1))
        def _():
            stream(1, UP, taken.at[0, UP], s).start()

        @pl.when((z == DEPTH - 1) & (x_hi == 0) & (s < PIECES - 1))
        def _():
            stream(1, UP, psi_hbm, s + 1).start()

    def weigh(k, j):
        half_across(k, j).wait_recv()
        whole = gram[k, j, mine, :] + half_in[k, j].astype(jnp.float32)
        scaled = whole * slab[k, mine, columns(j)].astype(jnp.float32)
        weight[k, j, mine, :] = scaled.astype(jnp.bfloat16)
        weight_ahead(k, j).start()
        weight_to_sibling(k, j).start()

    def add_own(k, j):
        weight_to_sibling(k, j).wait_recv()
        for n in range(4):
            part = pl.ds(n * (width // 4), width // 4)
            total[:, part] += contract(
                weight[k, j], taken[k, DOWN, columns(j), part], ((1,), (0,))
            )

    def step(i, carry):
        j, k = i // 2, i % 2
        for h in range(PIECES // CHUNKS):
            s = j * (PIECES // CHUNKS) + h
            arrival(k, DOWN, s).wait_recv()

            @pl.when(k == 0)
            def _():
                arrival(0, UP, s).wait_recv()
                turn(s)

        gram[k, j] = contract(own[...], taken[k, DOWN, columns(j), :], ((1,), (1,)))
        gram_to_sibling(k, j).start()

        @pl.when(i >= 1)
        def _():
            weigh((i + 1) % 2, (i + 1) // 2 - 1)

        gram_to_sibling(k, j).wait_recv()
        mine_now = gram[k, j, mine, :] + gram_in[k, j]
        gram[k, j, mine, :] = mine_now
        half_out[k, j] = mine_now.astype(jnp.bfloat16)
        half_across(k, j).start()

        @pl.when(i >= 2)
        def _():
            add_own(k, j - 1)

        return carry

    lax.fori_loop(0, 2 * CHUNKS, step, 0)
    weigh(1, CHUNKS - 1)

    def last_own(k, carry):
        add_own(k, CHUNKS - 1)
        return carry

    lax.fori_loop(0, 2, last_own, 0)

    def pass_on(i, carry):
        weight_ahead(i % 2, i // 2).wait_recv()
        weight_on(i % 2, i // 2).start()
        return carry

    def finish(j, carry):
        def partner(k, inner):
            weight_on(k, j).wait_recv()
            for n in range(4):
                part = pl.ds(n * (width // 4), width // 4)
                total[columns(j), part] += contract(
                    weight_in[k, j], taken[k, UP, :, part], ((0,), (0,))
                )
            return inner

        lax.fori_loop(0, 2, partner, 0)
        result[columns(j), :] = total[columns(j), :].astype(jnp.bfloat16)
        pltpu.make_async_copy(
            result.at[columns(j)], out_hbm.at[columns(j)], store_sem.at[j]
        ).start()
        return carry

    lax.fori_loop(0, 2 * CHUNKS - 2, pass_on, 0)
    for s in range(PIECES):
        arrival(1, UP, s).wait_recv()
    lax.fori_loop(0, CHUNKS - 2, finish, 0)
    lax.fori_loop(2 * CHUNKS - 2, 2 * CHUNKS, pass_on, 0)
    lax.fori_loop(CHUNKS - 2, CHUNKS, finish, 0)

    for offset in range(2):
        for way in (DOWN, UP):
            for s in range(PIECES):
                stream(offset, way, psi_hbm, s).wait_send()

    def drain(i, carry):
        k, j = i % 2, i // 2
        for sent in (gram_to_sibling, half_across, weight_to_sibling, weight_ahead, weight_on):
            sent(k, j).wait_send()
        return carry

    lax.fori_loop(0, 2 * CHUNKS, drain, 0)
    for j in range(CHUNKS):
        pltpu.make_async_copy(
            result.at[columns(j)], out_hbm.at[columns(j)], store_sem.at[j]
        ).wait()


def solution(mesh):
    blocks = mesh.shape["blk"]

    def per_device(orbitals, coulomb_near, coulomb_far):
        rows, width = orbitals.shape
        chunk, half = rows // CHUNKS, rows // 2
        chunked = (2, CHUNKS)
        return pl.pallas_call(
            functools.partial(kernel, blocks),
            out_shape=jax.ShapeDtypeStruct((rows, width), jnp.bfloat16),
            in_specs=[pl.BlockSpec(memory_space=pl.ANY)] * 3,
            out_specs=pl.BlockSpec(memory_space=pl.ANY),
            scratch_shapes=[
                pltpu.VMEM((rows, width), jnp.bfloat16),
                pltpu.VMEM((2, 2, rows, width), jnp.bfloat16),
                pltpu.VMEM((2, rows, rows), jnp.bfloat16),
                pltpu.VMEM((*chunked, rows, chunk), jnp.float32),
                pltpu.VMEM((*chunked, half, chunk), jnp.float32),
                pltpu.VMEM((*chunked, half, chunk), jnp.bfloat16),
                pltpu.VMEM((*chunked, half, chunk), jnp.bfloat16),
                pltpu.VMEM((*chunked, rows, chunk), jnp.bfloat16),
                pltpu.VMEM((*chunked, rows, chunk), jnp.bfloat16),
                pltpu.VMEM((rows, width), jnp.float32),
                pltpu.VMEM((rows, width), jnp.bfloat16),
                pltpu.SemaphoreType.DMA((3,)),
                pltpu.SemaphoreType.DMA((CHUNKS,)),
                pltpu.SemaphoreType.DMA((2, 2, PIECES)),
                pltpu.SemaphoreType.DMA((2, 2, PIECES)),
                pltpu.SemaphoreType.DMA((5, *chunked)),
                pltpu.SemaphoreType.DMA((5, *chunked)),
            ],
            compiler_params=pltpu.CompilerParams(
                collective_id=0, has_side_effects=True, vmem_limit_bytes=48 << 20
            ),
        )(orbitals, coulomb_near, coulomb_far)

    return jax.shard_map(
        per_device,
        mesh=mesh,
        in_specs=(P("blk", "orb"), P("blk", None), P("blk", None)),
        out_specs=P("blk", "orb"),
        check_vma=False,
    )
```

time: 249 us -> 103 us (0.41)
  waiting for transfers between devices: 200 us -> 0 us
  Pallas kernels: 0 us -> 97.6 us
  matrix products: 17 us -> 0 us
  starting transfers between devices: 15.5 us -> 0 us
  between operations: 13.5 us -> 0.01 us
  local copies, waits for them, and re-layouts: 1.36 us -> 4.99 us
    psum x1 -> x0, waiting for transfers between devices: 140 us -> none  [per_device(): lax.psum(contract(orbitals, psi, ((1,), (1,))), 'orb')]
    pallas_call x0 -> x1, Pallas kernels: none -> 97.6 us  [per_device(): pl.pallas_call(functools.partial(kernel, blocks), out_shape=jax.ShapeDtyp...]
    ppermute x6 -> x0, waiting for transfers between devices: 60.2 us -> none  [from_behind(): lax.ppermute(value, axis, [(i, (i + by) % devices) for i in range(devices)])]
    dot_general x6 -> x0, matrix products: 17 us -> none  [contract(): lax.dot_general(left, right, (dims, ((), ())), preferred_element_type=jnp...]
    ppermute x6 -> x0, starting transfers between devices: 15.5 us -> none  [from_behind(): lax.ppermute(value, axis, [(i, (i + by) % devices) for i in range(devices)])]
    unnamed x14 -> x7, local copies, waits for them, and re-layouts: 1.36 us -> 4.99 us
  transfers between devices with their start and end apart: 7 -> 0, of which waited for: 4 -> 0; matrix products, arithmetic and copies ran while one was open for 5% -> 0% of each run, Pallas kernels for 0% -> 0%
where the time goes in v2:
time: 103 us
  Pallas kernels  97.6 us (95%)
  local copies, waits for them, and re-layouts  4.99 us (5%)
    pallas_call x1, Pallas kernels, per_device(): pl.pallas_call(functools.partial(kernel, blocks), out_shape=jax.ShapeDtyp...  97.6 us
    unnamed x7, local copies, waits for them, and re-layouts  4.99 us

profile of v2, /device:TPU:1, one launch (start us, length us, event | category | flops | bytes accessed | tf_op | source)
XLA Modules:
  0.0 102.6 jit_solution(10184747765022577910)
XLA Ops:
  0.0 0.0 copy-start
  0.0 1.6 %copy-done = bf16[512,2048]{1,0:T(8,128)(2,1)S(1)} copy-done((bf16[512,2048]{1,0:T(8,128)(2,1)S(1)}, bf16[512,2048]{1,0:T(8,128)(2,1)}, u32[]{:S(2)}) %copy-start) | copy-done | bytes 2097176
  1.6 0.0 copy-start.1
  1.6 1.0 %copy-done.1 = bf16[512,512]{1,0:T(8,128)(2,1)S(1)} copy-done((bf16[512,512]{1,0:T(8,128)(2,1)S(1)}, bf16[512,512]{1,0:T(8,128)(2,1)}, u32[]{:S(2)}) %copy-start.1) | copy-done | bytes 524312
  2.6 0.0 copy-start.2
  2.6 1.0 %copy-done.2 = bf16[512,512]{1,0:T(8,128)(2,1)S(1)} copy-done((bf16[512,512]{1,0:T(8,128)(2,1)S(1)}, bf16[512,512]{1,0:T(8,128)(2,1)}, u32[]{:S(2)}) %copy-start.2) | copy-done | bytes 524312
  3.7 97.6 %shard_map.37 = bf16[512,2048]{1,0:T(8,128)(2,1)S(1)} custom-call(bf16[512,2048]{1,0:T(8,128)(2,1)S(1)} %copy-done, bf16[512,512]{1,0:T(8,128)(2,1)S(1)} %copy-done.1, bf16[512,512]{1,0:T(8,128)(2,1)S(1)} %copy-done.2), custom_call_target="tpu_custom_call" | custom-call | tf_op jit(solution)/shard_map/pallas_call | solution.py:278
  101.3 1.3 %copy.5 = bf16[512,2048]{1,0:T(8,128)(2,1)} copy(bf16[512,2048]{1,0:T(8,128)(2,1)S(1)} %shard_map.37) | data formatting | bytes 4194304
Async XLA Ops:
  0.0 1.6 %copy-start = (bf16[512,2048]{1,0:T(8,128)(2,1)S(1)}, bf16[512,2048]{1,0:T(8,128)(2,1)}, u32[]{:S(2)}) copy-start(bf16[512,2048]{1,0:T(8,128)(2,1)} %psi_hbm.1) | copy-start | bytes 6291460
  1.6 1.0 %copy-start.1 = (bf16[512,512]{1,0:T(8,128)(2,1)S(1)}, bf16[512,512]{1,0:T(8,128)(2,1)}, u32[]{:S(2)}) copy-start(bf16[512,512]{1,0:T(8,128)(2,1)} %near_hbm.1) | copy-start | bytes 1572868
  2.6 1.0 %copy-start.2 = (bf16[512,512]{1,0:T(8,128)(2,1)S(1)}, bf16[512,512]{1,0:T(8,128)(2,1)}, u32[]{:S(2)}) copy-start(bf16[512,512]{1,0:T(8,128)(2,1)} %far_hbm.1) | copy-start | bytes 1572868

commit v3 on v2

--- a/solution.py
+++ b/solution.py
@@ -8,7 +8,9 @@
 from jax.sharding import PartitionSpec as P
 
 MESH = pl.DeviceIdType.MESH
-PIECES = 8
+PIECES = 16
+LEAD = 2
+STRAIGHT = 2
 CHUNKS = 4
 FAR = 16
 DEPTH = 8
@@ -60,7 +62,9 @@
     other = pl.ds(pl.multiple_of((1 - core) * half, half), half)
 
     def stream(offset, way, source, s):
-        target = ((behind[0], ahead[0]), (near_down, near_up))[offset][way]
+        straight = isinstance(s, int) and s >= PIECES - STRAIGHT
+        near = (behind[1], ahead[1]) if straight else (near_down, near_up)
+        target = ((behind[0], ahead[0]), near)[offset][way]
         part = pl.ds(pl.multiple_of(s * piece, piece), piece)
         return pltpu.make_async_remote_copy(
             src_ref=source.at[part],
@@ -125,46 +129,35 @@
         pl.semaphore_signal(barrier, inc=1, device_id=peer, device_id_type=MESH)
     pl.semaphore_wait(barrier, len(peers))
 
+    for s in range(PIECES - STRAIGHT, PIECES):
+
+        @pl.when((z == 0) & (x_hi == 0))
+        def _():
+            stream(1, DOWN, psi_hbm, s).start()
+
+        @pl.when((z == DEPTH - 1) & (x_hi == 1))
+        def _():
+            stream(1, UP, psi_hbm, s).start()
+
     for s in range(PIECES):
         stream(0, DOWN, psi_hbm, s).start()
         stream(0, UP, psi_hbm, s).start()
 
-        @pl.when(z > 0)
+        @pl.when((z > 0) | (x_hi == 1))
         def _():
             stream(1, DOWN, psi_hbm, s).start()
 
-        @pl.when(z < DEPTH - 1)
+        @pl.when((z < DEPTH - 1) | (x_hi == 0))
         def _():
             stream(1, UP, psi_hbm, s).start()
-
-    @pl.when((z == 0) & (x_hi == 1))
-    def _():
-        stream(1, DOWN, psi_hbm, 0).start()
-
-    @pl.when((z == DEPTH - 1) & (x_hi == 0))
-    def _():
-        stream(1, UP, psi_hbm, 0).start()
 
     total[...] = jnp.zeros_like(total)
     for load in loads:
         load.wait()
 
-    def turn(s):
-        @pl.when((z == 0) & (x_hi == 0))
-        def _():
-            stream(1, DOWN, taken.at[0, DOWN], s).start()
-
-        @pl.when((z == 0) & (x_hi == 1) & (s < PIECES - 1))
-        def _():
-            stream(1, DOWN, psi_hbm, s + 1).start()
-
-        @pl.when((z == DEPTH - 1) & (x_hi == 1))
-        def _():
-            stream(1, UP, taken.at[0, UP], s).start()
-
-        @pl.when((z == DEPTH - 1) & (x_hi == 0) & (s < PIECES - 1))
-        def _():
-            stream(1, UP, psi_hbm, s + 1).start()
+    def forward_up(s):
+        arrival(0, UP, s).wait_recv()
+        stream(1, UP, taken.at[0, UP], s).start()
 
     def weigh(k, j):
         half_across(k, j).wait_recv()
@@ -175,30 +168,50 @@
         weight_to_sibling(k, j).start()
 
     def add_own(k, j):
+        weight_to_sibling(k, j - 1).wait_recv()
         weight_to_sibling(k, j).wait_recv()
+        left = jnp.concatenate([weight[k, j - 1], weight[k, j]], axis=1)
+        span = pl.ds(pl.multiple_of((j - 1) * chunk, chunk), 2 * chunk)
         for n in range(4):
             part = pl.ds(n * (width // 4), width // 4)
-            total[:, part] += contract(
-                weight[k, j], taken[k, DOWN, columns(j), part], ((1,), (0,))
-            )
+            total[:, part] += contract(left, taken[k, DOWN, span, part], ((1,), (0,)))
+
+    per = PIECES // CHUNKS
+    ends = low + high
+
+    def event(i):
+        return i % 2, i // 2
 
     def step(i, carry):
-        j, k = i // 2, i % 2
-        for h in range(PIECES // CHUNKS):
-            s = j * (PIECES // CHUNKS) + h
+        k, j = event(i)
+
+        @pl.when((k == 0) & (high * x_hi == 1))
+        def _():
+            @pl.when(j == 0)
+            def _():
+                for s in range(LEAD):
+                    forward_up(s)
+
+            for h in range(per):
+
+                @pl.when(j * per + LEAD + h < PIECES - STRAIGHT)
+                def _():
+                    forward_up(j * per + LEAD + h)
+
+        for h in range(per):
+            s = j * per + h
             arrival(k, DOWN, s).wait_recv()
 
-            @pl.when(k == 0)
+            @pl.when((k == 0) & (low * (1 - x_hi) == 1) & (s < PIECES - STRAIGHT))
             def _():
-                arrival(0, UP, s).wait_recv()
-                turn(s)
+                stream(1, DOWN, taken.at[0, DOWN], s).start()
 
         gram[k, j] = contract(own[...], taken[k, DOWN, columns(j), :], ((1,), (1,)))
         gram_to_sibling(k, j).start()
 
-        @pl.when(i >= 1)
-        def _():
-            weigh((i + 1) % 2, (i + 1) // 2 - 1)
+        @pl.when((i >= 1) & (ends == 0))
+        def _():
+            weigh(*event(i - 1))
 
         gram_to_sibling(k, j).wait_recv()
         mine_now = gram[k, j, mine, :] + gram_in[k, j]
@@ -206,49 +219,68 @@
         half_out[k, j] = mine_now.astype(jnp.bfloat16)
         half_across(k, j).start()
 
-        @pl.when(i >= 2)
-        def _():
-            add_own(k, j - 1)
+        @pl.when((i >= 2) & (event(i - 2)[1] % 2 == 1) & (ends == 0))
+        def _():
+            add_own(*event(i - 2))
 
         return carry
 
     lax.fori_loop(0, 2 * CHUNKS, step, 0)
-    weigh(1, CHUNKS - 1)
-
-    def last_own(k, carry):
-        add_own(k, CHUNKS - 1)
-        return carry
-
-    lax.fori_loop(0, 2, last_own, 0)
+    def close(i, carry):
+        @pl.when(i < 2 * CHUNKS)
+        def _():
+            weigh(*event(i))
+
+        @pl.when((i >= 1) & (event(i - 1)[1] % 2 == 1))
+        def _():
+            add_own(*event(i - 1))
+
+        return carry
+
+    lax.fori_loop((1 - ends) * (2 * CHUNKS - 1), 2 * CHUNKS + 1, close, 0)
 
     def pass_on(i, carry):
         weight_ahead(i % 2, i // 2).wait_recv()
         weight_on(i % 2, i // 2).start()
         return carry
 
-    def finish(j, carry):
-        def partner(k, inner):
-            weight_on(k, j).wait_recv()
-            for n in range(4):
-                part = pl.ds(n * (width // 4), width // 4)
-                total[columns(j), part] += contract(
-                    weight_in[k, j], taken[k, UP, :, part], ((0,), (0,))
-                )
-            return inner
-
-        lax.fori_loop(0, 2, partner, 0)
-        result[columns(j), :] = total[columns(j), :].astype(jnp.bfloat16)
-        pltpu.make_async_copy(
-            result.at[columns(j)], out_hbm.at[columns(j)], store_sem.at[j]
-        ).start()
+    def block_rows(m):
+        return pl.ds(pl.multiple_of(m * 2 * chunk, 2 * chunk), 2 * chunk)
+
+    def store(m):
+        return pltpu.make_async_copy(
+            result.at[block_rows(m)], out_hbm.at[block_rows(m)], store_sem.at[m]
+        )
+
+    def finish(m, carry):
+        lefts = []
+        for k in range(2):
+            weight_on(k, 2 * m).wait_recv()
+            weight_on(k, 2 * m + 1).wait_recv()
+            lefts.append(jnp.concatenate([weight_in[k, 2 * m], weight_in[k, 2 * m + 1]], axis=1))
+        for n in range(4):
+            part = pl.ds(n * (width // 4), width // 4)
+            value = total[block_rows(m), part]
+            for k in range(2):
+                value += contract(lefts[k], taken[k, UP, :, part], ((0,), (0,)))
+            result[block_rows(m), part] = value.astype(jnp.bfloat16)
+        store(m).start()
         return carry
 
     lax.fori_loop(0, 2 * CHUNKS - 2, pass_on, 0)
     for s in range(PIECES):
         arrival(1, UP, s).wait_recv()
-    lax.fori_loop(0, CHUNKS - 2, finish, 0)
+        if s < PIECES - STRAIGHT:
+
+            @pl.when(high * x_hi == 0)
+            def _():
+                arrival(0, UP, s).wait_recv()
+
+        else:
+            arrival(0, UP, s).wait_recv()
+    lax.fori_loop(0, CHUNKS // 2 - 1, finish, 0)
     lax.fori_loop(2 * CHUNKS - 2, 2 * CHUNKS, pass_on, 0)
-    lax.fori_loop(CHUNKS - 2, CHUNKS, finish, 0)
+    lax.fori_loop(CHUNKS // 2 - 1, CHUNKS // 2, finish, 0)
 
     for offset in range(2):
         for way in (DOWN, UP):
@@ -262,10 +294,8 @@
         return carry
 
     lax.fori_loop(0, 2 * CHUNKS, drain, 0)
-    for j in range(CHUNKS):
-        pltpu.make_async_copy(
-            result.at[columns(j)], out_hbm.at[columns(j)], store_sem.at[j]
-        ).wait()
+    for m in range(CHUNKS // 2):
+        store(m).wait()
 
 
 def solution(mesh):
@@ -293,14 +323,14 @@
                 pltpu.VMEM((rows, width), jnp.float32),
                 pltpu.VMEM((rows, width), jnp.bfloat16),
                 pltpu.SemaphoreType.DMA((3,)),
-                pltpu.SemaphoreType.DMA((CHUNKS,)),
+                pltpu.SemaphoreType.DMA((CHUNKS // 2,)),
                 pltpu.SemaphoreType.DMA((2, 2, PIECES)),
                 pltpu.SemaphoreType.DMA((2, 2, PIECES)),
                 pltpu.SemaphoreType.DMA((5, *chunked)),
                 pltpu.SemaphoreType.DMA((5, *chunked)),
             ],
             compiler_params=pltpu.CompilerParams(
-                collective_id=0, has_side_effects=True, vmem_limit_bytes=48 << 20
+                collective_id=0, has_side_effects=True, vmem_limit_bytes=67043328
             ),
         )(orbitals, coulomb_near, coulomb_far)
 

time: 103 us -> 85.6 us (0.83)
  Pallas kernels: 97.6 us -> 82.3 us
  local copies, waits for them, and re-layouts: 4.99 us -> 3.16 us
    pallas_call x1, Pallas kernels: 97.6 us -> 82.3 us  [per_device(): pl.pallas_call(functools.partial(kernel, blocks), out_shape=jax.ShapeDtyp...]
    unnamed x7 -> x1, local copies, waits for them, and re-layouts: 4.99 us -> 3.16 us
where the time goes in v3:
time: 85.6 us; the launch traced here: 85.5 us
  Pallas kernels  82.3 us (96%)
  local copies, waits for them, and re-layouts  3.16 us (4%)
    pallas_call x1, Pallas kernels, per_device(): pl.pallas_call(functools.partial(kernel, blocks), out_shape=jax.ShapeDtyp...  82.3 us
    unnamed x1, local copies, waits for them, and re-layouts  3.16 us

profile of v3, /device:TPU:1, one launch (start us, length us, event | category | flops | bytes accessed | tf_op | source)
XLA Modules:
  0.0 85.5 jit_solution(8680789904857423593)
XLA Ops:
  0.0 82.3 %shard_map.37 = bf16[512,2048]{1,0:T(8,128)(2,1)} custom-call(bf16[512,2048]{1,0:T(8,128)(2,1)} %psi_hbm.1, bf16[512,512]{1,0:T(8,128)(2,1)} %near_hbm.1, bf16[512,512]{1,0:T(8,128)(2,1)} %far_hbm.1), custom_call_target="tpu_custom_call" | custom-call | tf_op jit(solution)/shard_map/pallas_call | solution.py:308
  82.3 3.2 %copy.5 = bf16[512,2048]{1,0:T(8,128)(2,1)} copy(bf16[512,2048]{1,0:T(8,128)(2,1)} %shard_map.37) | data formatting | bytes 4194304

commit v4 on v3

--- a/solution.py
+++ b/solution.py
@@ -26,7 +26,7 @@
     psi_hbm,
     near_hbm,
     far_hbm,
-    out_hbm,
+    out_ref,
     own,
     taken,
     slab,
@@ -37,9 +37,7 @@
     weight,
     weight_in,
     total,
-    result,
     load_sem,
-    store_sem,
     psi_send,
     psi_recv,
     pair_send,
@@ -247,11 +245,6 @@
     def block_rows(m):
         return pl.ds(pl.multiple_of(m * 2 * chunk, 2 * chunk), 2 * chunk)
 
-    def store(m):
-        return pltpu.make_async_copy(
-            result.at[block_rows(m)], out_hbm.at[block_rows(m)], store_sem.at[m]
-        )
-
     def finish(m, carry):
         lefts = []
         for k in range(2):
@@ -263,8 +256,7 @@
             value = total[block_rows(m), part]
             for k in range(2):
                 value += contract(lefts[k], taken[k, UP, :, part], ((0,), (0,)))
-            result[block_rows(m), part] = value.astype(jnp.bfloat16)
-        store(m).start()
+            out_ref[block_rows(m), part] = value.astype(jnp.bfloat16)
         return carry
 
     lax.fori_loop(0, 2 * CHUNKS - 2, pass_on, 0)
@@ -294,8 +286,6 @@
         return carry
 
     lax.fori_loop(0, 2 * CHUNKS, drain, 0)
-    for m in range(CHUNKS // 2):
-        store(m).wait()
 
 
 def solution(mesh):
@@ -309,7 +299,7 @@
             functools.partial(kernel, blocks),
             out_shape=jax.ShapeDtypeStruct((rows, width), jnp.bfloat16),
             in_specs=[pl.BlockSpec(memory_space=pl.ANY)] * 3,
-            out_specs=pl.BlockSpec(memory_space=pl.ANY),
+            out_specs=pl.BlockSpec(memory_space=pltpu.VMEM),
             scratch_shapes=[
                 pltpu.VMEM((rows, width), jnp.bfloat16),
                 pltpu.VMEM((2, 2, rows, width), jnp.bfloat16),
@@ -321,18 +311,16 @@
                 pltpu.VMEM((*chunked, rows, chunk), jnp.bfloat16),
                 pltpu.VMEM((*chunked, rows, chunk), jnp.bfloat16),
                 pltpu.VMEM((rows, width), jnp.float32),
-                pltpu.VMEM((rows, width), jnp.bfloat16),
                 pltpu.SemaphoreType.DMA((3,)),
-                pltpu.SemaphoreType.DMA((CHUNKS // 2,)),
                 pltpu.SemaphoreType.DMA((2, 2, PIECES)),
                 pltpu.SemaphoreType.DMA((2, 2, PIECES)),
                 pltpu.SemaphoreType.DMA((5, *chunked)),
                 pltpu.SemaphoreType.DMA((5, *chunked)),
             ],
             compiler_params=pltpu.CompilerParams(
-                collective_id=0, has_side_effects=True, vmem_limit_bytes=67043328
+                collective_id=0, has_side_effects=True, vmem_limit_bytes=48 << 20
             ),
-        )(orbitals, coulomb_near, coulomb_far)
+        )(*[pltpu.with_memory_space_constraint(v, pltpu.HBM) for v in (orbitals, coulomb_near, coulomb_far)])
 
     return jax.shard_map(
         per_device,

time: 85.6 us -> 82.9 us (0.968)
  local copies, waits for them, and re-layouts: 3.16 us -> 1.32 us
    unnamed x1, local copies, waits for them, and re-layouts: 3.16 us -> 1.32 us
where the time goes in v4:
time: 82.9 us
  Pallas kernels  81.5 us (98%)
  local copies, waits for them, and re-layouts  1.32 us (2%)
    pallas_call x1, Pallas kernels, per_device(): pl.pallas_call(functools.partial(kernel, blocks), out_shape=jax.ShapeDtyp...  81.5 us

profile of v4, /device:TPU:1, one launch (start us, length us, event | category | flops | bytes accessed | tf_op | source)
XLA Modules:
  0.0 82.9 jit_solution(917257486924227934)
XLA Ops:
  0.0 81.5 %shard_map.37 = bf16[512,2048]{1,0:T(8,128)(2,1)S(1)} custom-call(bf16[512,2048]{1,0:T(8,128)(2,1)} %psi_hbm.1, bf16[512,512]{1,0:T(8,128)(2,1)} %near_hbm.1, bf16[512,512]{1,0:T(8,128)(2,1)} %far_hbm.1), custom_call_target="tpu_custom_call" | custom-call | tf_op jit(solution)/shard_map/pallas_call | solution.py:298
  81.5 1.3 %copy.5 = bf16[512,2048]{1,0:T(8,128)(2,1)} copy(bf16[512,2048]{1,0:T(8,128)(2,1)S(1)} %shard_map.37) | data formatting | bytes 4194304

commit v5 on v4

--- a/solution.py
+++ b/solution.py
@@ -10,7 +10,7 @@
 MESH = pl.DeviceIdType.MESH
 PIECES = 16
 LEAD = 2
-STRAIGHT = 2
+STRAIGHT = (0, 2)
 CHUNKS = 4
 FAR = 16
 DEPTH = 8
@@ -42,6 +42,7 @@
     psi_recv,
     pair_send,
     pair_recv,
+    ready,
 ):
     rows, width = own.shape
     piece, chunk, half = rows // PIECES, rows // CHUNKS, rows // 2
@@ -60,7 +61,7 @@
     other = pl.ds(pl.multiple_of((1 - core) * half, half), half)
 
     def stream(offset, way, source, s):
-        straight = isinstance(s, int) and s >= PIECES - STRAIGHT
+        straight = isinstance(s, int) and s >= PIECES - STRAIGHT[way]
         near = (behind[1], ahead[1]) if straight else (near_down, near_up)
         target = ((behind[0], ahead[0]), near)[offset][way]
         part = pl.ds(pl.multiple_of(s * piece, piece), piece)
@@ -122,16 +123,28 @@
         load.start()
 
     barrier = pltpu.get_barrier_semaphore()
-    peers = (sibling, across, ahead[0], behind[0], ahead[1], behind[1], near_down, near_up)
-    for peer in peers:
+    for peer in (sibling, across, ahead[0], behind[0], near_down, behind[1]):
         pl.semaphore_signal(barrier, inc=1, device_id=peer, device_id_type=MESH)
-    pl.semaphore_wait(barrier, len(peers))
-
-    for s in range(PIECES - STRAIGHT, PIECES):
-
-        @pl.when((z == 0) & (x_hi == 0))
-        def _():
-            stream(1, DOWN, psi_hbm, s).start()
+
+    @pl.when(z < DEPTH - 1)
+    def _():
+        for peer in (near_up, ahead[1]):
+            pl.semaphore_signal(barrier, inc=1, device_id=peer, device_id_type=MESH)
+
+    @pl.when(z == 0)
+    def _():
+        pl.semaphore_wait(barrier, 6)
+
+    @pl.when(z > 0)
+    def _():
+        pl.semaphore_wait(barrier, 8)
+
+    @pl.when(z == DEPTH - 1)
+    def _():
+        for peer in (near_up, ahead[1]):
+            pl.semaphore_signal(ready, inc=1, device_id=peer, device_id_type=MESH)
+
+    for s in range(PIECES - STRAIGHT[UP], PIECES):
 
         @pl.when((z == DEPTH - 1) & (x_hi == 1))
         def _():
@@ -141,13 +154,28 @@
         stream(0, DOWN, psi_hbm, s).start()
         stream(0, UP, psi_hbm, s).start()
 
-        @pl.when((z > 0) | (x_hi == 1))
+        @pl.when(z > 0)
         def _():
             stream(1, DOWN, psi_hbm, s).start()
 
         @pl.when((z < DEPTH - 1) | (x_hi == 0))
         def _():
             stream(1, UP, psi_hbm, s).start()
+
+    @pl.when(z == 0)
+    def _():
+        pl.semaphore_wait(ready, 2)
+        for s in range(PIECES - STRAIGHT[DOWN], PIECES):
+
+            @pl.when(x_hi == 0)
+            def _():
+                stream(1, DOWN, psi_hbm, s).start()
+
+        for s in range(PIECES):
+
+            @pl.when(x_hi == 1)
+            def _():
+                stream(1, DOWN, psi_hbm, s).start()
 
     total[...] = jnp.zeros_like(total)
     for load in loads:
@@ -178,29 +206,32 @@
     ends = low + high
 
     def event(i):
-        return i % 2, i // 2
+        late = i // (2 * CHUNKS - 4) * ends
+        k = (1 - late) * (i % 2) + late * (i % 4 // 2)
+        j = (1 - late) * (i // 2) + late * (CHUNKS - 2 + i % 2)
+        return (k + high) % 2, j
 
     def step(i, carry):
         k, j = event(i)
 
-        @pl.when((k == 0) & (high * x_hi == 1))
-        def _():
-            @pl.when(j == 0)
+        @pl.when((i % 2 == 0) & (high * x_hi == 1))
+        def _():
+            @pl.when(i == 0)
             def _():
                 for s in range(LEAD):
                     forward_up(s)
 
             for h in range(per):
 
-                @pl.when(j * per + LEAD + h < PIECES - STRAIGHT)
+                @pl.when(i // 2 * per + LEAD + h < PIECES - STRAIGHT[UP])
                 def _():
-                    forward_up(j * per + LEAD + h)
+                    forward_up(i // 2 * per + LEAD + h)
 
         for h in range(per):
             s = j * per + h
             arrival(k, DOWN, s).wait_recv()
 
-            @pl.when((k == 0) & (low * (1 - x_hi) == 1) & (s < PIECES - STRAIGHT))
+            @pl.when((k == 0) & (low * (1 - x_hi) == 1) & (s < PIECES - STRAIGHT[DOWN]))
             def _():
                 stream(1, DOWN, taken.at[0, DOWN], s).start()
 
@@ -229,13 +260,21 @@
         def _():
             weigh(*event(i))
 
-        @pl.when((i >= 1) & (event(i - 1)[1] % 2 == 1))
+        @pl.when((i >= 1) & (event(i - 1)[1] % 2 == 1) & (ends == 0))
         def _():
             add_own(*event(i - 1))
 
         return carry
 
     lax.fori_loop((1 - ends) * (2 * CHUNKS - 1), 2 * CHUNKS + 1, close, 0)
+
+    @pl.when(ends == 1)
+    def _():
+        def own_last(i, carry):
+            add_own(i % 2, i // 2 * 2 + 1)
+            return carry
+
+        lax.fori_loop(0, CHUNKS, own_last, 0)
 
     def pass_on(i, carry):
         weight_ahead(i % 2, i // 2).wait_recv()
@@ -262,7 +301,7 @@
     lax.fori_loop(0, 2 * CHUNKS - 2, pass_on, 0)
     for s in range(PIECES):
         arrival(1, UP, s).wait_recv()
-        if s < PIECES - STRAIGHT:
+        if s < PIECES - STRAIGHT[UP]:
 
             @pl.when(high * x_hi == 0)
             def _():
@@ -316,6 +355,7 @@
                 pltpu.SemaphoreType.DMA((2, 2, PIECES)),
                 pltpu.SemaphoreType.DMA((5, *chunked)),
                 pltpu.SemaphoreType.DMA((5, *chunked)),
+                pltpu.SemaphoreType.REGULAR,
             ],
             compiler_params=pltpu.CompilerParams(
                 collective_id=0, has_side_effects=True, vmem_limit_bytes=48 << 20

time: 82.9 us -> 82.3 us (level)
  no operation moved by 1% of the time
where the time goes in v5:
time: 82.3 us; the launch traced here: 82.2 us
  Pallas kernels  80.9 us (98%)
  local copies, waits for them, and re-layouts  1.32 us (2%)
    pallas_call x1, Pallas kernels, per_device(): pl.pallas_call(functools.partial(kernel, blocks), out_shape=jax.ShapeDtyp...  80.9 us

profile of v5, /device:TPU:1, one launch (start us, length us, event | category | flops | bytes accessed | tf_op | source)
XLA Modules:
  0.0 82.2 jit_solution(6747866700544721832)
XLA Ops:
  0.0 80.9 %shard_map.37 = bf16[512,2048]{1,0:T(8,128)(2,1)S(1)} custom-call(bf16[512,2048]{1,0:T(8,128)(2,1)} %psi_hbm.1, bf16[512,512]{1,0:T(8,128)(2,1)} %near_hbm.1, bf16[512,512]{1,0:T(8,128)(2,1)} %far_hbm.1), custom_call_target="tpu_custom_call" | custom-call | tf_op jit(solution)/shard_map/pallas_call | solution.py:337
  80.9 1.3 %copy.5 = bf16[512,2048]{1,0:T(8,128)(2,1)} copy(bf16[512,2048]{1,0:T(8,128)(2,1)S(1)} %shard_map.37) | data formatting | bytes 4194304

commit v6 on v5

--- a/solution.py
+++ b/solution.py
@@ -10,7 +10,7 @@
 MESH = pl.DeviceIdType.MESH
 PIECES = 16
 LEAD = 2
-STRAIGHT = (0, 2)
+STRAIGHT = (0, 1)
 CHUNKS = 4
 FAR = 16
 DEPTH = 8

time: 82.3 us -> 85.9 us (1.044)
  the two profiles are of different devices: /device:TPU:1 before, /device:TPU:5 now
where the time goes in v6:
time: 85.9 us; the launch traced here: 85.8 us
  Pallas kernels  84.5 us (98%)
  local copies, waits for them, and re-layouts  1.32 us (2%)
    pallas_call x1, Pallas kernels, per_device(): pl.pallas_call(functools.partial(kernel, blocks), out_shape=jax.ShapeDtyp...  84.5 us

profile of v6, /device:TPU:5, one launch (start us, length us, event | category | flops | bytes accessed | tf_op | source)
XLA Modules:
  0.0 85.8 jit_solution(8030827369185143009)
XLA Ops:
  0.0 84.5 %shard_map.37 = bf16[512,2048]{1,0:T(8,128)(2,1)S(1)} custom-call(bf16[512,2048]{1,0:T(8,128)(2,1)} %psi_hbm.1, bf16[512,512]{1,0:T(8,128)(2,1)} %near_hbm.1, bf16[512,512]{1,0:T(8,128)(2,1)} %far_hbm.1), custom_call_target="tpu_custom_call" | custom-call | tf_op jit(solution)/shard_map/pallas_call | solution.py:337
  84.5 1.3 %copy.5 = bf16[512,2048]{1,0:T(8,128)(2,1)} copy(bf16[512,2048]{1,0:T(8,128)(2,1)S(1)} %shard_map.37) | data formatting | bytes 4194304
